TPU v7x, 512 devices: a whole 4x4x16 slice. The times are simulated.
512 devices in a mesh: dp: 16 (over z), expert: 32 (over y, x, core).
Axes of the slice: x: 4, y: 4, z: 16, core: 2. Of those that a mesh axis runs over, the one named last changes fastest.
Arguments:
- tokens: bfloat16 [2048, 4096], P('dp', 'expert'), may hold values from -6 to 6
- norm_gain: float32 [4096], replicated, may hold values from 0.1 to 1.9
- routes: int32 [2048, 2], P('dp'), may hold values from 0 to 31, all different within a row; in each aligned block of 128 rows (0 to 127, 128 to 255, ...) at most 10 rows name the same one
- route_prob: float32 [2048, 2], P('dp'), may hold values from 0.2 to 1
- gate_weight: bfloat16 [32, 4096, 2048], P('expert', None, 'dp'), may hold values from -0.09375 to 0.09375
- up_weight: bfloat16 [32, 4096, 2048], P('expert', None, 'dp'), may hold values from -0.09375 to 0.09375
- down_weight: bfloat16 [32, 2048, 4096], P('expert', 'dp'), may hold values from -0.125 to 0.125
- key_value_weight: bfloat16 [4096, 2048], P('expert'), may hold values from -0.09375 to 0.09375
- key_value_target: bfloat16 [2048, 2048], P('dp', 'expert'), may hold values from -6 to 6
- concept_mask: int32 [2048], P('dp'), may hold values 0 or 1
Outputs:
- down_grad: bfloat16 [32, 2048, 4096], P('expert', 'dp')
- key_value_grad: float32 [4096, 2048], P('expert', 'dp')
Inputs may be any that keep to these rules, and one draw needn't show every extreme that they name: `routes`: in each aligned block of 128 rows no expert is named by more than 10 rows; the two choices of a token differ.
All inputs are finite; a program needn't handle non-finite values. No bound on the sum of `concept_mask` on one device may be relied on, other than what follows from the above.
Results may differ from a plain program's by a relative error of at most 0.033.
Values may be sent and summed in bfloat16 or wider, within the bound.
No kernel may reach another device: no remote copies, remote signals or barrier semaphores. Data moves between devices by JAX's collectives and lax.ppermute only.
A program may use at most 64 MiB of HBM per device.

v0:
```python
import jax
import jax.numpy as jnp
from jax import lax
from jax.sharding import PartitionSpec as P

eps_norm = 1e-06


def slot_targets(routes, expert_count, capacity):
    flat = routes.reshape(-1)
    onehot = (flat[:, None] == jnp.arange(expert_count, dtype=jnp.int32)[None, :]).astype(jnp.int32)
    before = jnp.cumsum(onehot, axis=0) - onehot
    return flat * capacity + jnp.sum(before * onehot, axis=1)


def per_device(
    tokens,
    norm_gain,
    routes,
    route_prob,
    gate_weight,
    up_weight,
    down_weight,
    key_value_weight,
    key_value_target,
    concept_mask,
):
    token_rows, width = tokens.shape
    top_count = routes.shape[1]
    expert_count = lax.axis_size("expert")
    capacity = 5 * token_rows * top_count // (4 * expert_count)
    model_width = width * expert_count
    position = slot_targets(routes, expert_count, capacity)
    prob_flat = route_prob.reshape(-1)

    def place_rows(pair_rows):
        filled = (
            jnp.zeros((expert_count * capacity, width), jnp.bfloat16).at[position].set(pair_rows)
        )
        return filled.reshape(expert_count, capacity, width)

    values = tokens.astype(jnp.float32)
    total_sq = lax.psum(jnp.sum(values * values, axis=1), "expert")
    scale = lax.rsqrt(total_sq / model_width + eps_norm)
    local_gain = lax.dynamic_slice_in_dim(norm_gain, lax.axis_index("expert") * width, width)
    outgoing = (values * scale[:, None] * local_gain[None, :]).astype(jnp.bfloat16)
    send_slots = place_rows(jnp.repeat(outgoing, top_count, axis=0))
    arrived = lax.all_to_all(send_slots, "expert", split_axis=0, concat_axis=2, tiled=True)[0]
    rows = lax.all_gather(arrived, "dp", axis=0, tiled=True)
    gate_val = jnp.dot(rows, gate_weight[0], preferred_element_type=jnp.float32)
    up_val = jnp.dot(rows, up_weight[0], preferred_element_type=jnp.float32)
    hidden = (jax.nn.silu(gate_val) * up_val).astype(jnp.bfloat16)
    expert_out = lax.psum_scatter(
        jnp.dot(hidden, down_weight[0], preferred_element_type=jnp.float32).astype(jnp.bfloat16),
        "dp",
        scatter_dimension=0,
        tiled=True,
    )
    returned = lax.all_to_all(expert_out[None], "expert", split_axis=2, concat_axis=0, tiled=True)
    picked = returned.reshape(expert_count * capacity, width)[position].astype(jnp.float32)
    expert_mix = (picked * prob_flat[:, None]).reshape(token_rows, top_count, width).sum(axis=1)
    state = (tokens.astype(jnp.float32) + expert_mix).astype(jnp.bfloat16)
    proj_term = jnp.dot(state, key_value_weight, preferred_element_type=jnp.float32)
    proj_cols = lax.psum_scatter(
        proj_term.astype(jnp.bfloat16), "expert", scatter_dimension=1, tiled=True
    ).astype(jnp.float32)
    mask_col = concept_mask.astype(jnp.float32)[:, None]
    cotangent_cols = (
        mask_col * (proj_cols - key_value_target.astype(jnp.float32)) * token_rows ** (-0.5)
    ).astype(jnp.bfloat16)
    cotangent = lax.all_gather(cotangent_cols, "expert", axis=1, tiled=True)
    grad_term = jnp.einsum("tw,tk->wk", state, cotangent, preferred_element_type=jnp.float32)
    key_value_grad = lax.psum_scatter(
        grad_term.astype(jnp.bfloat16), "dp", scatter_dimension=1, tiled=True
    ).astype(jnp.float32)
    state_grad = jnp.einsum(
        "tk,wk->tw", cotangent, key_value_weight, preferred_element_type=jnp.float32
    )
    pair_grad = (jnp.repeat(state_grad, top_count, axis=0) * prob_flat[:, None]).astype(
        jnp.bfloat16
    )
    grad_slots = place_rows(pair_grad)
    landed = lax.all_to_all(grad_slots, "expert", split_axis=0, concat_axis=2, tiled=True)[0]
    down_total = jnp.einsum(
        "rf,rd->fd",
        hidden,
        lax.all_gather(landed, "dp", axis=0, tiled=True),
        preferred_element_type=jnp.float32,
    )
    return (down_total.astype(jnp.bfloat16)[None], key_value_grad)


def solution(mesh):
    placed = (
        P("dp", "expert"),
        P(),
        P("dp", None),
        P("dp", None),
        P("expert", None, "dp"),
        P("expert", None, "dp"),
        P("expert", "dp", None),
        P("expert", None),
        P("dp", "expert"),
        P("dp"),
    )
    return jax.shard_map(
        per_device,
        mesh=mesh,
        in_specs=placed,
        out_specs=(P("expert", "dp", None), P("expert", "dp")),
        check_vma=False,
    )
```

profile of v0, /device:TPU:2, one launch (start us, length us, event | category | flops | bytes accessed | tf_op | source)
XLA Modules:
  0.0 632.4 jit_solution(2933031377896465025)
XLA Ops:
  7.2 0.0 copy-start
  7.2 0.0 all-gather.5.cloned.1.call-start
  7.2 0.8 broadcast_multiply_fusion
  8.0 0.8 copy.34
  8.8 0.1 eq.29
  8.9 0.1 eq.25
  9.1 0.9 fusion.7
  9.9 63.0 %psum.7 = f32[128]{0:T(128)S(1)} all-reduce(f32[128]{0:T(128)S(1)} %fusion.7), channel_id=1, replica_groups=mesh['dp'=16,'expert'=32] {'expert'}, use_global_device_ids=true, to_apply=%region_4.5 | all-reduce | flops 128 | bytes 1024 | tf_op jit(solution)/shard_map/psum | solution.py:43
  72.9 0.1 copy.33
  73.0 0.1 mul.83
  73.2 0.6 reduce-window.6
  73.8 0.2 slice_reduce_fusion
  74.0 0.8 dynamic_slice.3
  74.8 0.8 fusion.9
  75.6 0.1 fusion.18
  75.8 1.2 scatter_custom_fusion
  77.0 14.9 %all_to_all.45 = bf16[32,10,128]{2,1,0:T(8,128)(2,1)S(1)} all-to-all(bf16[32,10,128]{2,1,0:T(8,128)(2,1)S(1)} %reshape.83), channel_id=1, replica_groups=mesh['dp'=16,'expert'=32] {'expert'}, dimensions={0} | all-to-all | bytes 163840 | tf_op jit(solution)/shard_map/all_to_all | solution.py:48
  92.0 0.7 reshape.112
  92.7 0.0 all-gather.5.cloned.1.call-update
  92.7 0.0 all-reduce.3.cloned.1.call-start
  92.8 74.1 %all-gather.5.cloned.1.call-done = bf16[16,10,4096]{2,1,0:T(8,128)(2,1)} async-done(((bf16[1,10,4096]{2,1,0:T(8,128)(2,1)}), bf16[16,10,4096]{2,1,0:T(8,128)(2,1)}) %all-gather.5.cloned.1.call-update) | async-done | bytes 1310736 | tf_op jit(solution)/shard_map/all_gather | solution.py:49
  166.9 1.8 reshape.113
  168.7 0.5 fusion.4
  169.2 0.7 copy-done.3
  170.0 0.5 fusion.1
  170.5 1.6 convolution_convert_fusion
  172.1 0.0 all-reduce.3.cloned.1.call-update
  172.1 0.1 copy.41
  172.2 1.3 dynamic-slice
  174.1 135.3 %all-reduce.3.cloned.1.call-done = bf16[160,4096]{1,0:T(8,128)(2,1)} async-done(((bf16[160,4096]{1,0:T(8,128)(2,1)}), bf16[160,4096]{1,0:T(8,128)(2,1)}) %all-reduce.3.cloned.1.call-update) | async-done | bytes 1310736
  309.4 1.0 dynamic-slice_bitcast_fusion
  310.4 2.8 copy.38
  313.2 0.5 broadcast.74
  313.7 23.4 %reduce.2 = bf16[4096,10]{1,0:T(8,128)(2,1)} reduce(bf16[4096,1,10]{2,1,0:T(2,128)(2,1)S(1)} %bitcast.74, bf16[]{:T(256)} %broadcast.74), dimensions={1}, to_apply=%bitcast.60.reduce_sub_computation | reduce | bytes 163842
  337.1 3.4 reshape.126
  340.5 7.4 %all-to-all-start.1 = ((bf16[32,2,640]{2,1,0:T(2,128)(2,1)}), bf16[32,2,640]{2,1,0:T(2,128)(2,1)S(1)}, u32[]{:S(2)}, u32[]{:S(2)}) async-start(bf16[32,2,640]{2,1,0:T(2,128)(2,1)} %reshape.126), calls=%async_computation.1 | async-start | bytes 163840 | tf_op jit(solution)/shard_map/all_to_all | solution.py:59
  348.0 0.0 reduce-scatter.5.cloned.1.call-start
  348.0 6.3 all-to-all-done.1
  354.3 2.2 reshape.127
  356.6 2.1 copy.39
  358.9 0.9 gather_fusion
  359.7 0.2 fusion.6
  360.0 1.1 convolution_convert_fusion.3
  361.1 0.0 reduce-scatter.5.cloned.1.call-update
  361.2 0.0 reduce-scatter.7.cloned.1.call-start
  361.2 93.7 %reduce-scatter.5.cloned.1.call-done = bf16[128,64]{0,1:T(8,128)(2,1)} async-done(((bf16[128,2048]{0,1:T(8,128)(2,1)}), bf16[128,64]{0,1:T(8,128)(2,1)}) %reduce-scatter.5.cloned.1.call-update) | async-done | bytes 16400 | tf_op jit(solution)/shard_map/reduce_scatter | solution.py:64
  455.0 0.7 multiply_convert_fusion.2
  455.7 23.2 %all_gather.10 = bf16[128,2048]{0,1:T(8,128)(2,1)S(1)} all-gather(bf16[128,64]{0,1:T(8,128)(2,1)S(1)} %multiply_convert_fusion.2), channel_id=1, replica_groups=mesh['dp'=16,'expert'=32] {'expert'}, dimensions={1}, use_global_device_ids=true | all-gather | bytes 540672 | tf_op jit(solution)/shard_map/all_gather | solution.py:71
  478.9 0.3 convolution_convert_fusion.2
  479.2 1.0 copy.44
  480.2 0.0 reduce-scatter.7.cloned.1.call-update
  480.2 0.0 all-gather.7.cloned.1.call-start
  480.3 0.1 mul.99
  480.4 0.3 fusion.22
  480.8 1.3 scatter_custom_fusion.1
  482.1 12.6 %all_to_all.46 = bf16[32,10,128]{2,1,0:T(8,128)(2,1)S(1)} all-to-all(bf16[32,10,128]{2,1,0:T(8,128)(2,1)S(1)} %reshape.86), channel_id=1, replica_groups=mesh['dp'=16,'expert'=32] {'expert'}, dimensions={0} | all-to-all | bytes 163840 | tf_op jit(solution)/shard_map/all_to_all | solution.py:83
  494.7 0.7 reshape.114
  495.4 0.0 all-gather.7.cloned.1.call-update
  495.4 54.2 %reduce-scatter.7.cloned.1.call-done = bf16[128,128]{1,0:T(8,128)(2,1)} async-done(((bf16[2048,128]{1,0:T(8,128)(2,1)}), bf16[128,128]{1,0:T(8,128)(2,1)}) %reduce-scatter.7.cloned.1.call-update) | async-done | bytes 32784
  549.6 0.9 copy.45
  550.5 0.6 convert_element_type.74
  551.1 71.5 %all-gather.7.cloned.1.call-done = bf16[16,10,4096]{2,1,0:T(8,128)(2,1)} async-done(((bf16[1,10,4096]{2,1,0:T(8,128)(2,1)}), bf16[16,10,4096]{2,1,0:T(8,128)(2,1)}) %all-gather.7.cloned.1.call-update) | async-done | bytes 1310736 | tf_op jit(solution)/shard_map/all_gather | solution.py:87
  622.7 1.8 reshape.115
  624.5 1.4 fusion
  (31 shorter events, 0.4 us)
Async XLA Ops:
  7.2 163.3 %copy-start = (bf16[1,128,4096]{2,1,0:T(8,128)(2,1)S(1)}, bf16[1,128,4096]{2,1,0:T(8,128)(2,1)}, u32[]{:S(2)}) copy-start(bf16[1,128,4096]{2,1,0:T(8,128)(2,1)} %param.16) | copy-start | bytes 3145732
  7.2 159.7 %all-gather.5.cloned.1.call-start = ((), (), s32[]{:S(2)}) async-start(), calls=%async_computation.6 | async-start | bytes 2228224 | tf_op jit(solution)/shard_map/all_gather | solution.py:49
  92.7 76.0 %copy-start.2 = (bf16[1,4096,128]{2,1,0:T(8,128)(2,1)S(1)}, bf16[1,4096,128]{2,1,0:T(8,128)(2,1)}, u32[]{:S(2)}) copy-start(bf16[1,4096,128]{2,1,0:T(8,128)(2,1)} %param.14) | copy-start | bytes 3145732
  92.7 216.7 %all-reduce.3.cloned.1.call-start = ((), (), s32[]{:S(2)}) async-start(), calls=%async_computation.9 | async-start | bytes 2621440
  168.7 1.2 copy-start.3
  170.5 1.6 copy-start.6
  340.5 13.8 %all-to-all-start.1 = ((bf16[32,2,640]{2,1,0:T(2,128)(2,1)}), bf16[32,2,640]{2,1,0:T(2,128)(2,1)S(1)}, u32[]{:S(2)}, u32[]{:S(2)}) async-start(bf16[32,2,640]{2,1,0:T(2,128)(2,1)} %reshape.126), calls=%async_computation.1 | async-start | bytes 163840 | tf_op jit(solution)/shard_map/all_to_all | solution.py:59
  348.0 107.0 %reduce-scatter.5.cloned.1.call-start = ((), (), s32[]{:S(2)}) async-start(), calls=%async_computation.5 | async-start | bytes 540672 | tf_op jit(solution)/shard_map/reduce_scatter | solution.py:64
  358.7 1.3 copy-start.1
  358.7 1.3 copy-start.4
  358.8 2.4 copy-start.7
  358.8 96.2 %copy-start.5 = (bf16[128,64]{0,1:T(8,128)(2,1)S(1)}, bf16[128,64]{0,1:T(8,128)(2,1)}, u32[]{:S(2)}) copy-start(bf16[128,64]{0,1:T(8,128)(2,1)} %param.18) | copy-start | bytes 49156
  361.2 188.5 %reduce-scatter.7.cloned.1.call-start = ((), (), s32[]{:S(2)}) async-start(), calls=%async_computation.8 | async-start | bytes 557056
  480.2 142.4 %all-gather.7.cloned.1.call-start = ((), (), s32[]{:S(2)}) async-start(), calls=%async_computation.7 | async-start | bytes 2228224 | tf_op jit(solution)/shard_map/all_gather | solution.py:87
Sparse Core Ops, SparseCore 0:
  92.8 74.0 all-gather.4
  172.2 137.1 all-reduce.2
  361.3 93.6 reduce-scatter.4
  480.3 69.2 reduce-scatter.6
  551.8 70.8 all-gather.6
where the time goes:
time: 633 us; the launch traced here: 632 us
  waiting for transfers between devices  435 us (69%)
  blocking collectives  114 us (18%)
  other arithmetic  29.5 us (5%)
  local copies, waits for them, and re-layouts  25.8 us (4%)
  between operations  14.8 us (2%)
  starting transfers between devices  7.63 us (1%)
    unnamed x7, waiting for transfers between devices  190 us
    reduce_scatter x1, waiting for transfers between devices, per_device(): lax.psum_scatter(proj_term.astype(jnp.bfloat16), 'expert', scatter_dimens...  93.7 us
    all_gather x1, waiting for transfers between devices, per_device(): rows = lax.all_gather(arrived, 'dp', axis=0, tiled=True)  74.1 us
    all_gather x1, waiting for transfers between devices, per_device(): lax.all_gather(landed, 'dp', axis=0, tiled=True)  71.5 us
    psum x1, blocking collectives, per_device(): total_sq = lax.psum(jnp.sum(values * values, axis=1), 'expert')  63 us
    unnamed x1, other arithmetic  23.4 us
    all_gather x1, blocking collectives, per_device(): cotangent = lax.all_gather(cotangent_cols, 'expert', axis=1, tiled=True)  23.2 us
    unnamed x29, local copies, waits for them, and re-layouts  16 us
  transfers between devices with their start and end apart: 6, of which 6 were waited for; matrix products, arithmetic and copies ran while one was open for 1% of the time, Pallas kernels for 0%

commit v1 on v0

--- a/solution.py
+++ b/solution.py
@@ -1,9 +1,28 @@
+import functools
 import jax
 import jax.numpy as jnp
 from jax import lax
 from jax.sharding import PartitionSpec as P
 
 eps_norm = 1e-06
+
+
+def put_the_thing(my_data, pos_dim):
+    axis_len = lax.axis_size("dp")
+    pages = []
+    for no in range(1, axis_len):
+        pages.append((no - 1, no))
+    all_values = my_data
+    y = pages + [(axis_len - 1, 0)]
+    crops = [all_values]
+    for _ in range(axis_len - 1):
+        all_values = lax.ppermute(all_values, "dp", y)
+        crops += [all_values]
+    small = jnp.concatenate([*reversed(crops)], pos_dim)
+    return jnp.roll(small, (lax.axis_index("dp") + 1) * all_values.shape[pos_dim], pos_dim)
+
+
+roads_track = functools.partial(put_the_thing, pos_dim=0)
 
 
 def slot_targets(routes, expert_count, capacity):
@@ -46,7 +65,7 @@
     outgoing = (values * scale[:, None] * local_gain[None, :]).astype(jnp.bfloat16)
     send_slots = place_rows(jnp.repeat(outgoing, top_count, axis=0))
     arrived = lax.all_to_all(send_slots, "expert", split_axis=0, concat_axis=2, tiled=True)[0]
-    rows = lax.all_gather(arrived, "dp", axis=0, tiled=True)
+    rows = roads_track(arrived)
     gate_val = jnp.dot(rows, gate_weight[0], preferred_element_type=jnp.float32)
     up_val = jnp.dot(rows, up_weight[0], preferred_element_type=jnp.float32)
     hidden = (jax.nn.silu(gate_val) * up_val).astype(jnp.bfloat16)

time: 633 us -> 760 us (1.20)
  local copies, waits for them, and re-layouts: 25.8 us -> 92.6 us
  starting transfers between devices: 7.63 us -> 37.8 us
  waiting for transfers between devices: 435 us -> 459 us
    ppermute x0 -> x15, waiting for transfers between devices: none -> 99.6 us  [put_the_thing(): all_values = lax.ppermute(all_values, 'dp', y)]
    all_gather x1 -> x0, waiting for transfers between devices: 74.1 us -> none  [per_device(): rows = lax.all_gather(arrived, 'dp', axis=0, tiled=True)]
    concatenate x0 -> x1, local copies, waits for them, and re-layouts: none -> 67.9 us  [put_the_thing(): jnp.roll(small, (lax.axis_index('dp') + 1) * all_values.shape[pos_dim], p...]
    ppermute x0 -> x15, starting transfers between devices: none -> 30 us  [put_the_thing(): all_values = lax.ppermute(all_values, 'dp', y)]
    unnamed x7 -> x6, waiting for transfers between devices: 190 us -> 188 us
    unnamed x29 -> x35, local copies, waits for them, and re-layouts: 16 us -> 14.9 us
  transfers between devices with their start and end apart: 6 -> 20, of which waited for: 6 -> 20; matrix products, arithmetic and copies ran while one was open for 1% -> 1% of each run, Pallas kernels for 0% -> 0%
where the time goes in v1:
time: 760 us; the launch traced here: 756 us
  waiting for transfers between devices  459 us (60%)
  blocking collectives  114 us (15%)
  local copies, waits for them, and re-layouts  92.6 us (12%)
  starting transfers between devices  37.8 us (5%)
  other arithmetic  29.4 us (4%)
  between operations  14.9 us (2%)
  matrix products  8.61 us (1%)
    unnamed x6, waiting for transfers between devices  188 us
    ppermute x15, waiting for transfers between devices, put_the_thing(): all_values = lax.ppermute(all_values, 'dp', y)  99.6 us
    reduce_scatter x1, waiting for transfers between devices, per_device(): lax.psum_scatter(proj_term.astype(jnp.bfloat16), 'expert', scatter_dimens...  93.7 us
    all_gather x1, waiting for transfers between devices, per_device(): lax.all_gather(landed, 'dp', axis=0, tiled=True)  71.6 us
    concatenate x1, local copies, waits for them, and re-layouts, put_the_thing(): jnp.roll(small, (lax.axis_index('dp') + 1) * all_values.shape[pos_dim], p...  67.9 us
    psum x1, blocking collectives, per_device(): total_sq = lax.psum(jnp.sum(values * values, axis=1), 'expert')  63 us
    ppermute x15, starting transfers between devices, put_the_thing(): all_values = lax.ppermute(all_values, 'dp', y)  30 us
    unnamed x1, other arithmetic  23.4 us
  transfers between devices with their start and end apart: 20, of which 20 were waited for; matrix products, arithmetic and copies ran while one was open for 1% of the time, Pallas kernels for 0%

profile of v1, /device:TPU:2, one launch (start us, length us, event | category | flops | bytes accessed | tf_op | source)
XLA Modules:
  0.0 756.4 jit_solution(8119767465460582902)
XLA Ops:
  7.2 0.9 copy.34
  9.1 0.9 fusion.9
  9.9 63.0 %psum.7 = f32[128]{0:T(128)S(1)} all-reduce(f32[128]{0:T(128)S(1)} %fusion.9), channel_id=1, replica_groups=mesh['dp'=16,'expert'=32] {'expert'}, use_global_device_ids=true, to_apply=%region_4.5 | all-reduce | flops 128 | bytes 1024 | tf_op jit(solution)/shard_map/psum | solution.py:62
  74.0 0.8 dynamic_slice.7
  74.8 0.8 fusion.11
  75.8 1.2 scatter_custom_fusion
  77.0 14.9 %all_to_all.45 = bf16[32,10,128]{2,1,0:T(8,128)(2,1)S(1)} all-to-all(bf16[32,10,128]{2,1,0:T(8,128)(2,1)S(1)} %reshape.83), channel_id=1, replica_groups=mesh['dp'=16,'expert'=32] {'expert'}, dimensions={0} | all-to-all | bytes 163840 | tf_op jit(solution)/shard_map/all_to_all | solution.py:67
  92.1 3.1 collective-permute-start
  95.2 11.4 %collective-permute-done = bf16[10,4096]{1,0:T(8,128)(2,1)S(1)} collective-permute-done((bf16[10,4096]{1,0:T(8,128)(2,1)S(1)}, bf16[10,4096]{1,0:T(8,128)(2,1)S(1)}, u32[]{:S(2)}, u32[]{:S(2)}) %collective-permute-start) | collective-permute-done | bytes 81952 | tf_op jit(solution)/shard_map/ppermute | solution.py:19
  106.5 1.9 collective-permute-start.1
  108.5 6.2 collective-permute-done.1
  114.7 1.9 collective-permute-start.2
  116.6 6.1 collective-permute-done.2
  122.7 1.9 collective-permute-start.3
  124.7 6.1 collective-permute-done.3
  130.8 1.9 collective-permute-start.4
  132.7 6.1 collective-permute-done.4
  138.9 1.9 collective-permute-start.5
  140.8 6.3 collective-permute-done.5
  147.0 1.9 collective-permute-start.6
  149.0 7.4 collective-permute-done.6
  156.4 1.9 collective-permute-start.7
  158.3 6.7 collective-permute-done.7
  165.0 1.9 collective-permute-start.8
  166.9 6.1 collective-permute-done.8
  173.1 1.9 collective-permute-start.9
  175.0 6.1 collective-permute-done.9
  181.1 1.9 collective-permute-start.10
  183.0 6.1 collective-permute-done.10
  189.8 1.9 collective-permute-start.11
  191.8 6.1 collective-permute-done.11
  198.6 1.9 collective-permute-start.12
  200.5 6.1 collective-permute-done.12
  207.3 1.9 collective-permute-start.13
  209.2 6.2 collective-permute-done.13
  215.4 2.1 collective-permute-start.14
  217.6 6.2 collective-permute-done.14
  223.8 67.9 %concatenate.6 = bf16[320,4096]{1,0:T(8,128)(2,1)} concatenate(bf16[10,4096]{1,0:T(8,128)(2,1)} %collective-permute-done.14, bf16[10,4096]{1,0:T(8,128)(2,1)} %collective-permute-done.13, bf16[10,4096]{1,0:T(8,128)(2,1)} %copy-done.7, bf16[10,4096]{1,0:T(8,128)(2,1)} %copy-done.6, bf16[10,4096]{1,0:T(8,128)(2,1)} %copy-done.5, bf16[10,4096]{1,0:T(8,128)(2,1)S(1)} %collective-permute-done.9, ...), dimensions={0} | concatenate | bytes 5242880 | tf_op jit(solution)/shard_map/jit(_roll_dynamic)/concatenate | solution.py:22
  291.8 2.0 fusion.3
  293.7 1.9 multiply_convert_fusion.1
  295.6 1.6 convolution_convert_fusion
  297.3 1.3 dynamic-slice
  299.3 133.9 %all-reduce.3.cloned.1.call-done = bf16[160,4096]{1,0:T(8,128)(2,1)} async-done(((bf16[160,4096]{1,0:T(8,128)(2,1)}), bf16[160,4096]{1,0:T(8,128)(2,1)}) %all-reduce.3.cloned.1.call-update) | async-done | bytes 1310736
  433.2 1.0 dynamic-slice_bitcast_fusion
  434.2 2.8 copy.38
  437.5 23.4 %reduce.2 = bf16[4096,10]{1,0:T(8,128)(2,1)} reduce(bf16[4096,1,10]{2,1,0:T(2,128)(2,1)S(1)} %bitcast.76, bf16[]{:T(256)} %broadcast.74), dimensions={1}, to_apply=%bitcast.65.reduce_sub_computation | reduce | bytes 163842
  460.9 3.4 reshape.123
  464.3 7.6 %all-to-all-start.1 = ((bf16[32,2,640]{2,1,0:T(2,128)(2,1)}), bf16[32,2,640]{2,1,0:T(2,128)(2,1)S(1)}, u32[]{:S(2)}, u32[]{:S(2)}) async-start(bf16[32,2,640]{2,1,0:T(2,128)(2,1)} %reshape.123), calls=%async_computation.1 | async-start | bytes 163840 | tf_op jit(solution)/shard_map/all_to_all | solution.py:78
  472.0 6.3 all-to-all-done.1
  478.3 2.2 reshape.124
  480.6 2.1 copy.39
  482.9 0.9 gather_fusion
  484.0 1.1 convolution_convert_fusion.3
  485.2 93.7 %reduce-scatter.5.cloned.1.call-done = bf16[128,64]{0,1:T(8,128)(2,1)} async-done(((bf16[128,2048]{0,1:T(8,128)(2,1)}), bf16[128,64]{0,1:T(8,128)(2,1)}) %reduce-scatter.5.cloned.1.call-update) | async-done | bytes 16400 | tf_op jit(solution)/shard_map/reduce_scatter | solution.py:83
  579.0 0.7 multiply_convert_fusion.3
  579.7 23.1 %all_gather.6 = bf16[128,2048]{0,1:T(8,128)(2,1)S(1)} all-gather(bf16[128,64]{0,1:T(8,128)(2,1)S(1)} %multiply_convert_fusion.3), channel_id=1, replica_groups=mesh['dp'=16,'expert'=32] {'expert'}, dimensions={1}, use_global_device_ids=true | all-gather | bytes 540672 | tf_op jit(solution)/shard_map/all_gather | solution.py:90
  603.2 1.0 copy.44
  604.8 1.3 scatter_custom_fusion.1
  606.1 12.6 %all_to_all.46 = bf16[32,10,128]{2,1,0:T(8,128)(2,1)S(1)} all-to-all(bf16[32,10,128]{2,1,0:T(8,128)(2,1)S(1)} %reshape.86), channel_id=1, replica_groups=mesh['dp'=16,'expert'=32] {'expert'}, dimensions={0} | all-to-all | bytes 163840 | tf_op jit(solution)/shard_map/all_to_all | solution.py:102
  619.4 54.2 %reduce-scatter.7.cloned.1.call-done = bf16[128,128]{1,0:T(8,128)(2,1)} async-done(((bf16[2048,128]{1,0:T(8,128)(2,1)}), bf16[128,128]{1,0:T(8,128)(2,1)}) %reduce-scatter.7.cloned.1.call-update) | async-done | bytes 32784
  673.6 0.9 copy.45
  675.1 71.6 %all-gather.3.cloned.1.call-done = bf16[16,10,4096]{2,1,0:T(8,128)(2,1)} async-done(((bf16[1,10,4096]{2,1,0:T(8,128)(2,1)}), bf16[16,10,4096]{2,1,0:T(8,128)(2,1)}) %all-gather.3.cloned.1.call-update) | async-done | bytes 1310736 | tf_op jit(solution)/shard_map/all_gather | solution.py:106
  746.6 1.8 reshape.113
  748.4 1.4 fusion
  (65 shorter events, 7.8 us)
Async XLA Ops:
  7.2 288.4 %copy-start = (bf16[1,128,4096]{2,1,0:T(8,128)(2,1)S(1)}, bf16[1,128,4096]{2,1,0:T(8,128)(2,1)}, u32[]{:S(2)}) copy-start(bf16[1,128,4096]{2,1,0:T(8,128)(2,1)} %param.16) | copy-start | bytes 3145732
  7.2 426.0 %all-reduce.3.cloned.1.call-start = ((), (), s32[]{:S(2)}) async-start(), calls=%async_computation.8 | async-start | bytes 2621440
  92.1 14.5 %collective-permute-start = (bf16[10,4096]{1,0:T(8,128)(2,1)S(1)}, bf16[10,4096]{1,0:T(8,128)(2,1)S(1)}, u32[]{:S(2)}, u32[]{:S(2)}) collective-permute-start(bf16[10,4096]{1,0:T(8,128)(2,1)S(1)} %bitcast.79), channel_id=1, source_target_pairs={{0,32},{32,64},{64,96},{96,128},{128,160},{160,192},{192,224},{224... | collective-permute-start | bytes 245768 | tf_op jit(solution)/shard_map/ppermute | solution.py:19
  106.5 8.1 %collective-permute-start.1 = (bf16[10,4096]{1,0:T(8,128)(2,1)S(1)}, bf16[10,4096]{1,0:T(8,128)(2,1)S(1)}, u32[]{:S(2)}, u32[]{:S(2)}) collective-permute-start(bf16[10,4096]{1,0:T(8,128)(2,1)S(1)} %collective-permute-done), channel_id=1, source_target_pairs={{0,32},{32,64},{64,96},{96,128},{128,160},{160,192},{192,224},{224... | collective-permute-start | bytes 245768 | tf_op jit(solution)/shard_map/ppermute | solution.py:19
  114.7 8.1 %collective-permute-start.2 = (bf16[10,4096]{1,0:T(8,128)(2,1)S(1)}, bf16[10,4096]{1,0:T(8,128)(2,1)S(1)}, u32[]{:S(2)}, u32[]{:S(2)}) collective-permute-start(bf16[10,4096]{1,0:T(8,128)(2,1)S(1)} %collective-permute-done.1), channel_id=1, source_target_pairs={{0,32},{32,64},{64,96},{96,128},{128,160},{160,192},{192,224},{224... | collective-permute-start | bytes 245768 | tf_op jit(solution)/shard_map/ppermute | solution.py:19
  122.7 8.1 %collective-permute-start.3 = (bf16[10,4096]{1,0:T(8,128)(2,1)S(1)}, bf16[10,4096]{1,0:T(8,128)(2,1)S(1)}, u32[]{:S(2)}, u32[]{:S(2)}) collective-permute-start(bf16[10,4096]{1,0:T(8,128)(2,1)S(1)} %collective-permute-done.2), channel_id=1, source_target_pairs={{0,32},{32,64},{64,96},{96,128},{128,160},{160,192},{192,224},{224... | collective-permute-start | bytes 245768 | tf_op jit(solution)/shard_map/ppermute | solution.py:19
  130.8 8.1 %collective-permute-start.4 = (bf16[10,4096]{1,0:T(8,128)(2,1)S(1)}, bf16[10,4096]{1,0:T(8,128)(2,1)S(1)}, u32[]{:S(2)}, u32[]{:S(2)}) collective-permute-start(bf16[10,4096]{1,0:T(8,128)(2,1)S(1)} %collective-permute-done.3), channel_id=1, source_target_pairs={{0,32},{32,64},{64,96},{96,128},{128,160},{160,192},{192,224},{224... | collective-permute-start | bytes 245768 | tf_op jit(solution)/shard_map/ppermute | solution.py:19
  138.9 8.2 %collective-permute-start.5 = (bf16[10,4096]{1,0:T(8,128)(2,1)S(1)}, bf16[10,4096]{1,0:T(8,128)(2,1)S(1)}, u32[]{:S(2)}, u32[]{:S(2)}) collective-permute-start(bf16[10,4096]{1,0:T(8,128)(2,1)S(1)} %collective-permute-done.4), channel_id=1, source_target_pairs={{0,32},{32,64},{64,96},{96,128},{128,160},{160,192},{192,224},{224... | collective-permute-start | bytes 245768 | tf_op jit(solution)/shard_map/ppermute | solution.py:19
  147.0 9.3 %collective-permute-start.6 = (bf16[10,4096]{1,0:T(8,128)(2,1)S(1)}, bf16[10,4096]{1,0:T(8,128)(2,1)S(1)}, u32[]{:S(2)}, u32[]{:S(2)}) collective-permute-start(bf16[10,4096]{1,0:T(8,128)(2,1)S(1)} %collective-permute-done.5), channel_id=1, source_target_pairs={{0,32},{32,64},{64,96},{96,128},{128,160},{160,192},{192,224},{224... | collective-permute-start | bytes 245768 | tf_op jit(solution)/shard_map/ppermute | solution.py:19
  156.4 8.6 %collective-permute-start.7 = (bf16[10,4096]{1,0:T(8,128)(2,1)S(1)}, bf16[10,4096]{1,0:T(8,128)(2,1)S(1)}, u32[]{:S(2)}, u32[]{:S(2)}) collective-permute-start(bf16[10,4096]{1,0:T(8,128)(2,1)S(1)} %collective-permute-done.6), channel_id=1, source_target_pairs={{0,32},{32,64},{64,96},{96,128},{128,160},{160,192},{192,224},{224... | collective-permute-start | bytes 245768 | tf_op jit(solution)/shard_map/ppermute | solution.py:19
  165.0 8.1 %collective-permute-start.8 = (bf16[10,4096]{1,0:T(8,128)(2,1)S(1)}, bf16[10,4096]{1,0:T(8,128)(2,1)S(1)}, u32[]{:S(2)}, u32[]{:S(2)}) collective-permute-start(bf16[10,4096]{1,0:T(8,128)(2,1)S(1)} %collective-permute-done.7), channel_id=1, source_target_pairs={{0,32},{32,64},{64,96},{96,128},{128,160},{160,192},{192,224},{224... | collective-permute-start | bytes 245768 | tf_op jit(solution)/shard_map/ppermute | solution.py:19
  173.1 8.1 %collective-permute-start.9 = (bf16[10,4096]{1,0:T(8,128)(2,1)S(1)}, bf16[10,4096]{1,0:T(8,128)(2,1)S(1)}, u32[]{:S(2)}, u32[]{:S(2)}) collective-permute-start(bf16[10,4096]{1,0:T(8,128)(2,1)S(1)} %collective-permute-done.8), channel_id=1, source_target_pairs={{0,32},{32,64},{64,96},{96,128},{128,160},{160,192},{192,224},{224... | collective-permute-start | bytes 245768 | tf_op jit(solution)/shard_map/ppermute | solution.py:19
  181.1 8.1 %collective-permute-start.10 = (bf16[10,4096]{1,0:T(8,128)(2,1)S(1)}, bf16[10,4096]{1,0:T(8,128)(2,1)S(1)}, u32[]{:S(2)}, u32[]{:S(2)}) collective-permute-start(bf16[10,4096]{1,0:T(8,128)(2,1)S(1)} %collective-permute-done.9), channel_id=1, source_target_pairs={{0,32},{32,64},{64,96},{96,128},{128,160},{160,192},{192,224},{224... | collective-permute-start | bytes 245768 | tf_op jit(solution)/shard_map/ppermute | solution.py:19
  189.2 0.7 copy-start.5
  189.8 8.1 %collective-permute-start.11 = (bf16[10,4096]{1,0:T(8,128)(2,1)S(1)}, bf16[10,4096]{1,0:T(8,128)(2,1)S(1)}, u32[]{:S(2)}, u32[]{:S(2)}) collective-permute-start(bf16[10,4096]{1,0:T(8,128)(2,1)S(1)} %collective-permute-done.10), channel_id=1, source_target_pairs={{0,32},{32,64},{64,96},{96,128},{128,160},{160,192},{192,224},{224... | collective-permute-start | bytes 245768 | tf_op jit(solution)/shard_map/ppermute | solution.py:19
  197.9 0.7 copy-start.6
  198.6 8.1 %collective-permute-start.12 = (bf16[10,4096]{1,0:T(8,128)(2,1)S(1)}, bf16[10,4096]{1,0:T(8,128)(2,1)S(1)}, u32[]{:S(2)}, u32[]{:S(2)}) collective-permute-start(bf16[10,4096]{1,0:T(8,128)(2,1)S(1)} %collective-permute-done.11), channel_id=1, source_target_pairs={{0,32},{32,64},{64,96},{96,128},{128,160},{160,192},{192,224},{224... | collective-permute-start | bytes 245768 | tf_op jit(solution)/shard_map/ppermute | solution.py:19
  206.6 0.7 copy-start.7
  207.3 8.2 %collective-permute-start.13 = (bf16[10,4096]{1,0:T(8,128)(2,1)S(1)}, bf16[10,4096]{1,0:T(8,128)(2,1)}, u32[]{:S(2)}, u32[]{:S(2)}) collective-permute-start(bf16[10,4096]{1,0:T(8,128)(2,1)S(1)} %collective-permute-done.12), channel_id=1, source_target_pairs={{0,32},{32,64},{64,96},{96,128},{128,160},{160,192},{192,224},{224... | collective-permute-start | bytes 245768 | tf_op jit(solution)/shard_map/ppermute | solution.py:19
  215.4 8.4 %collective-permute-start.14 = (bf16[10,4096]{1,0:T(8,128)(2,1)}, bf16[10,4096]{1,0:T(8,128)(2,1)}, u32[]{:S(2)}, u32[]{:S(2)}) collective-permute-start(bf16[10,4096]{1,0:T(8,128)(2,1)} %collective-permute-done.13), channel_id=1, source_target_pairs={{0,32},{32,64},{64,96},{96,128},{128,160},{160,192},{192,224},{224... | collective-permute-start | bytes 245768 | tf_op jit(solution)/shard_map/ppermute | solution.py:19
  217.6 74.2 %copy-start.3 = (bf16[1,4096,128]{2,1,0:T(8,128)(2,1)S(1)}, bf16[1,4096,128]{2,1,0:T(8,128)(2,1)}, u32[]{:S(2)}) copy-start(bf16[1,4096,128]{2,1,0:T(8,128)(2,1)} %param.14) | copy-start | bytes 3145732
  291.7 2.0 copy-start.2
  295.6 1.6 copy-start.9
  464.3 14.0 %all-to-all-start.1 = ((bf16[32,2,640]{2,1,0:T(2,128)(2,1)}), bf16[32,2,640]{2,1,0:T(2,128)(2,1)S(1)}, u32[]{:S(2)}, u32[]{:S(2)}) async-start(bf16[32,2,640]{2,1,0:T(2,128)(2,1)} %reshape.123), calls=%async_computation.1 | async-start | bytes 163840 | tf_op jit(solution)/shard_map/all_to_all | solution.py:78
  472.0 107.0 %reduce-scatter.5.cloned.1.call-start = ((), (), s32[]{:S(2)}) async-start(), calls=%async_computation.5 | async-start | bytes 540672 | tf_op jit(solution)/shard_map/reduce_scatter | solution.py:83
  482.7 1.3 copy-start.1
  482.7 1.3 copy-start.4
  482.8 2.4 copy-start.10
  482.8 96.2 %copy-start.8 = (bf16[128,64]{0,1:T(8,128)(2,1)S(1)}, bf16[128,64]{0,1:T(8,128)(2,1)}, u32[]{:S(2)}) copy-start(bf16[128,64]{0,1:T(8,128)(2,1)} %param.18) | copy-start | bytes 49156
  485.2 188.4 %reduce-scatter.7.cloned.1.call-start = ((), (), s32[]{:S(2)}) async-start(), calls=%async_computation.7 | async-start | bytes 557056
  604.2 142.4 %all-gather.3.cloned.1.call-start = ((), (), s32[]{:S(2)}) async-start(), calls=%async_computation.6 | async-start | bytes 2228224 | tf_op jit(solution)/shard_map/all_gather | solution.py:106
Sparse Core Ops, SparseCore 0:
  297.3 135.8 all-reduce.2
  485.3 93.6 reduce-scatter.4
  604.3 69.2 reduce-scatter.6
  675.7 70.8 all-gather.2
